TPU v7x, 256 devices: a whole 4x4x8 slice. The times are simulated.
256 devices in a mesh: seq: 16 (over x_lo, z), mp: 8 (over y, core), dp: 2 (over x_hi).
Axes of the slice: x: 4 (x_hi: 2, x_lo: 2; x = x_hi * 2 + x_lo), y: 4, z: 8, core: 2. Of those that a mesh axis runs over, the one named last changes fastest.
Arguments:
- residual_in: bfloat16 [12288, 2048], P(('dp', 'seq')), parts along dimension 0, may hold values from -6 to 6
- queries: bfloat16 [12288, 2048], P(('dp', 'seq'), 'mp'), parts along dimension 0, may hold values from -30 to 30
- keys: bfloat16 [12288, 2048], P(('dp', 'seq'), 'mp'), parts along dimension 0, may hold values from -10 to 10
- values: bfloat16 [12288, 2048], P(('dp', 'seq'), 'mp'), parts along dimension 0, may hold values from -6 to 6
- w_out: bfloat16 [2048, 2048], P('mp', 'seq'), may hold values from -0.1875 to 0.1875
- conv_value: bfloat16 [2048, 2048], P('seq', 'mp'), may hold values from -0.125 to 0.125
- conv_gate: bfloat16 [2048, 2048], P('seq', 'mp'), may hold values from -0.125 to 0.125
- depth_kernel: float32 [31, 2048], P(None, 'mp'), may hold values from -2 to 2
- conv_out: bfloat16 [2048, 2048], P('mp', 'seq'), may hold values from -0.25 to 0.25
- ffn_in: bfloat16 [2048, 8192], P('seq', 'mp'), may hold values from -0.125 to 0.125
- ffn_down: bfloat16 [8192, 2048], P('mp', 'seq'), may hold values from -0.1875 to 0.1875
- ffn_mask: int32 [96, 64], P(('dp', 'seq'), 'mp'), parts along dimension 0, may hold values 0 or 1
Outputs:
- block_out: float32 [12288, 2048], P(('dp', 'seq', 'mp')), parts along dimension 0
There are 2 independent parts, one for each index of `dp`. A program takes and returns all parts, laid end to end along the dimension named above; an argument that names none is the same for every part. Nothing has to cross between parts.
All inputs are finite; a program needn't handle non-finite values. No bound on the sum of `ffn_mask` on one device may be relied on, other than what follows from the above.
Results may differ from a plain program's by a relative error of at most 0.017.
Values may be sent and summed in bfloat16 or wider, within the bound.
A program may use at most 128 MiB of HBM per device.

v0:
```python
import math
import jax
import jax.numpy as jnp
from jax import lax
from jax.sharding import PartitionSpec as P

HEAD_DIM = 128
norm_epsilon = 1e-05


def padded_2(value, sides, width):
    for axis, dim in sides:
        count, length = (lax.axis_size(axis), value.shape[dim])
        up = [(i, (i + 1) % count) for i in range(count - 1)]
        down = [(j, i) for i, j in up]
        last = lax.slice_in_dim(value, length - width, length, axis=dim)
        leading = lax.slice_in_dim(value, 0, width, axis=dim)
        before = lax.ppermute(last, axis, up)
        after = lax.ppermute(leading, axis, down)
        value = jnp.concatenate([before, value, after], axis=dim)
    return value


def layer_norm(stream):
    row_mean = jnp.mean(stream, axis=-1, keepdims=True)
    centered = stream - row_mean
    spread = jnp.mean(centered * centered, axis=-1, keepdims=True)
    return centered * lax.rsqrt(spread + norm_epsilon)


def accumulate_rows(left, weight_piece):
    return jnp.dot(left, weight_piece, preferred_element_type=jnp.float32)


def add_branch(stream, branch_part, factor):
    return stream + factor * lax.psum(branch_part.astype(jnp.bfloat16), "mp").astype(jnp.float32)


def on_device(
    residual_in,
    queries,
    keys,
    values,
    w_out,
    conv_value,
    conv_gate,
    depth_kernel,
    conv_out,
    ffn_in,
    ffn_down,
    ffn_mask,
):
    row_count = queries.shape[0]
    local_width = queries.shape[1]
    heads_here = local_width // HEAD_DIM
    score_scale = 1.0 / math.sqrt(HEAD_DIM)
    query_heads = queries.reshape(row_count, heads_here, HEAD_DIM)
    pieces = (
        lax.all_gather(keys, "seq", axis=0, tiled=True),
        lax.all_gather(values, "seq", axis=0, tiled=True),
    )
    running_max = jnp.full((row_count, heads_here), -1e30, jnp.float32)
    key_heads = pieces[0].reshape(pieces[0].shape[0], heads_here, HEAD_DIM)
    value_heads = pieces[1].reshape(pieces[1].shape[0], heads_here, HEAD_DIM)
    scores = (
        jnp.einsum("qhd,khd->qhk", query_heads, key_heads, preferred_element_type=jnp.float32)
        * score_scale
    )
    new_max = jnp.maximum(running_max, jnp.max(scores, axis=-1))
    exp_scores = jnp.exp(scores - new_max[..., None])
    running_sum = jnp.sum(exp_scores, axis=-1)
    weighted = jnp.einsum(
        "qhk,khd->qhd",
        exp_scores.astype(jnp.bfloat16),
        value_heads,
        preferred_element_type=jnp.float32,
    )
    weighted, running_max, running_sum = (weighted, new_max, running_sum)
    heads_out = (
        (weighted / running_sum[..., None]).reshape(row_count, local_width).astype(jnp.bfloat16)
    )
    attn_part = jnp.dot(
        heads_out,
        lax.all_gather(w_out, "seq", axis=1, tiled=True),
        preferred_element_type=jnp.float32,
    )
    share_count = row_count // lax.axis_size("mp")
    stream = residual_in.astype(jnp.float32)
    stream = add_branch(stream, attn_part, 1.0)
    norm_one = layer_norm(stream).astype(jnp.bfloat16)
    conv_width = conv_value.shape[1]
    pieces = (
        lax.all_gather(conv_value, "seq", axis=0, tiled=True),
        lax.all_gather(conv_gate, "seq", axis=0, tiled=True),
    )
    value_half = accumulate_rows(norm_one, pieces[0])
    gate_half = accumulate_rows(norm_one, pieces[1])
    gated_units = (value_half * jax.nn.sigmoid(gate_half)).astype(jnp.bfloat16)
    half_width = depth_kernel.shape[0] // 2
    padded = padded_2(gated_units, (("seq", 0),), half_width)
    depth_out = jnp.zeros((row_count, conv_width), jnp.float32)
    for tap_index in range(depth_kernel.shape[0]):
        depth_out = depth_out + depth_kernel[tap_index] * padded[
            tap_index : tap_index + row_count
        ].astype(jnp.float32)
    activated = jax.nn.silu(depth_out).astype(jnp.bfloat16)
    conv_part = jnp.dot(
        activated,
        lax.all_gather(conv_out, "seq", axis=1, tiled=True),
        preferred_element_type=jnp.float32,
    )
    stream = add_branch(stream, conv_part, 1.0)
    norm_two = layer_norm(stream).astype(jnp.bfloat16)
    pre_hidden = accumulate_rows(norm_two, lax.all_gather(ffn_in, "seq", axis=0, tiled=True))
    tile_count, block_count = ffn_mask.shape
    hidden = (
        jax.nn.silu(pre_hidden).reshape(tile_count, row_count // tile_count, block_count, -1)
        * ffn_mask.astype(jnp.float32)[:, None, :, None]
    )
    hidden = hidden.reshape(row_count, -1).astype(jnp.bfloat16)
    ffn_part = jnp.dot(
        hidden,
        lax.all_gather(ffn_down, "seq", axis=1, tiled=True),
        preferred_element_type=jnp.float32,
    )
    stream = add_branch(stream, ffn_part, 0.5)
    stream = lax.dynamic_slice_in_dim(stream, lax.axis_index("mp") * share_count, share_count, 0)
    return layer_norm(stream)


def solution(mesh):
    in_specs = (
        P(("dp", "seq"), None),
        P(("dp", "seq"), "mp"),
        P(("dp", "seq"), "mp"),
        P(("dp", "seq"), "mp"),
        P("mp", "seq"),
        P("seq", "mp"),
        P("seq", "mp"),
        P(None, "mp"),
        P("mp", "seq"),
        P("seq", "mp"),
        P("mp", "seq"),
        P(("dp", "seq"), "mp"),
    )
    out_specs = P(("dp", "seq", "mp"), None)
    return jax.shard_map(
        on_device, mesh=mesh, in_specs=in_specs, out_specs=out_specs, check_vma=False
    )
```

profile of v0, /device:TPU:2, one launch (start us, length us, event | category | flops | bytes accessed | tf_op | source)
XLA Modules:
  0.0 830.0 jit_solution(12674205064811095764)
XLA Ops:
  9.9 74.6 %all-gather.9.cloned.1.call-done = bf16[6144,256]{0,1:T(8,128)(2,1)} async-done(((bf16[384,256]{0,1:T(8,128)(2,1)}), bf16[6144,256]{0,1:T(8,128)(2,1)}) %all-gather.9.cloned.1.call-update) | async-done | bytes 3145744 | tf_op jit(solution)/shard_map/all_gather | solution.py:59
  84.5 11.3 %bitcast_reduce_fusion = (f32[384,2]{0,1:T(2,128)S(1)}, f32[2,6144,384]{2,1,0:T(8,128)}) fusion(bf16[6144,2,128]{0,2,1:T(8,128)(2,1)} %bitcast.85, bf16[384,256]{1,0:T(8,128)(2,1)S(1)} %copy-done), kind=kOutput, calls=%fused_computation.1 | convolution fusion | flops 1217395968 | bytes 22219776 | tf_op jit(solution)/shard_map/qhd,khd->qhk/dot_general | solution.py:66
  95.8 61.8 %all-gather.11.cloned.1.call-done = bf16[6144,256]{1,0:T(8,128)(2,1)} async-done(((bf16[384,256]{1,0:T(8,128)(2,1)}), bf16[6144,256]{1,0:T(8,128)(2,1)}) %all-gather.11.cloned.1.call-update) | async-done | bytes 3145744 | tf_op jit(solution)/shard_map/all_gather | solution.py:60
  157.6 4.7 copy.19
  162.3 9.4 %fusion.1 = f32[384,2]{0,1:T(2,128)S(1)} fusion(f32[2,6144,384]{2,1,0:T(8,128)} %get-tuple-element.41, f32[384,2]{0,1:T(2,128)S(1)} %broadcast_maximum_fusion), kind=kLoop, calls=%fused_computation.3 | loop fusion | flops 14155008 | bytes 18880512 | tf_op jit(solution)/shard_map/reduce_sum | solution.py:71
  171.7 10.8 %fusion.22 = bf16[384,2,128]{0,2,1:T(8,128)(2,1)S(1)} fusion(bf16[6144,2,128]{0,2,1:T(8,128)(2,1)} %bitcast.84, f32[2,6144,384]{2,1,0:T(8,128)} %get-tuple-element.41, f32[384,2]{0,1:T(2,128)S(1)} %broadcast_maximum_fusion, f32[384,2]{0,1:T(2,128)S(1)} %fusion.1), kind=kOutput, calls=%fused_computation.59 | convolution fusion | flops 1222311936 | bytes 22222848 | tf_op jit(solution)/shard_map/qhk,khd->qhd/dot_general | solution.py:72
  182.6 39.6 %all-gather.13.cloned.1.call-done = bf16[256,2048]{1,0:T(8,128)(2,1)} async-done(((bf16[256,128]{1,0:T(8,128)(2,1)}), bf16[256,2048]{1,0:T(8,128)(2,1)}) %all-gather.13.cloned.1.call-update) | async-done | bytes 1048592 | tf_op jit(solution)/shard_map/all_gather | solution.py:84
  222.2 3.0 convolution_convert_fusion.2
  227.4 67.0 %all-reduce.4.cloned.1.call-done = bf16[384,2048]{1,0:T(8,128)(2,1)} async-done(((bf16[384,2048]{1,0:T(8,128)(2,1)}), bf16[384,2048]{1,0:T(8,128)(2,1)}) %all-reduce.4.cloned.1.call-update) | async-done | bytes 1572880 | tf_op jit(solution)/shard_map/psum | solution.py:36
  294.4 2.0 fusion.7
  298.9 64.7 %all-gather.17.cloned.1.call-done = bf16[2048,256]{1,0:T(8,128)(2,1)} async-done(((bf16[128,256]{1,0:T(8,128)(2,1)}), bf16[2048,256]{1,0:T(8,128)(2,1)}) %all-gather.17.cloned.1.call-update) | async-done | bytes 1048592 | tf_op jit(solution)/shard_map/all_gather | solution.py:94
  363.6 3.0 fusion.14
  366.7 65.0 %all-gather.15.cloned.1.call-done = bf16[2048,256]{1,0:T(8,128)(2,1)} async-done(((bf16[128,256]{1,0:T(8,128)(2,1)}), bf16[2048,256]{1,0:T(8,128)(2,1)}) %all-gather.15.cloned.1.call-update) | async-done | bytes 1048592 | tf_op jit(solution)/shard_map/all_gather | solution.py:93
  431.6 2.4 fusion.18
  434.0 2.5 collective-permute-start
  436.5 5.5 collective-permute-start.1
  442.0 54.1 %all-gather.19.cloned.1.call-done = bf16[256,2048]{1,0:T(8,128)(2,1)} async-done(((bf16[256,128]{1,0:T(8,128)(2,1)}), bf16[256,2048]{1,0:T(8,128)(2,1)}) %all-gather.19.cloned.1.call-update) | async-done | bytes 1048592 | tf_op jit(solution)/shard_map/all_gather | solution.py:109
  496.1 10.9 %convolution_convert_fusion.1 = bf16[384,2048]{1,0:T(8,128)(2,1)} fusion(bf16[256,2048]{1,0:T(8,128)(2,1)} %all-gather.19.cloned.1.call-done, bf16[384,256]{1,0:T(8,128)(2,1)} %copy-done.6, bf16[15,256]{1,0:T(8,128)(2,1)S(1)} %collective-permute-done.1, bf16[15,256]{1,0:T(8,128)(2,1)S(1)} %collective-permute-done, f32[256]{0:T(256)S(1)} %bitcast.117, ...), kind=kOutput, calls=%fused_computation.15 | convolution fusion | flops 421822464 | bytes 2865152 | tf_op jit(solution)/shard_map/dot_general | solution.py:107
  508.4 67.8 %all-reduce.6.cloned.1.call-done = bf16[384,2048]{1,0:T(8,128)(2,1)} async-done(((bf16[384,2048]{1,0:T(8,128)(2,1)}), bf16[384,2048]{1,0:T(8,128)(2,1)}) %all-reduce.6.cloned.1.call-update) | async-done | bytes 1572880 | tf_op jit(solution)/shard_map/psum | solution.py:36
  576.2 2.1 fusion.61
  580.4 72.2 %all-gather.21.cloned.1.call-done = bf16[2048,1024]{1,0:T(8,128)(2,1)} async-done(((bf16[128,1024]{1,0:T(8,128)(2,1)}), bf16[2048,1024]{1,0:T(8,128)(2,1)}) %all-gather.21.cloned.1.call-update) | async-done | bytes 4194320 | tf_op jit(solution)/shard_map/all_gather | solution.py:114
  652.7 87.1 %all-gather.23.cloned.1.call-done = bf16[1024,2048]{1,0:T(8,128)(2,1)} async-done(((bf16[1024,128]{1,0:T(8,128)(2,1)}), bf16[1024,2048]{1,0:T(8,128)(2,1)}) %all-gather.23.cloned.1.call-update) | async-done | bytes 4194320 | tf_op jit(solution)/shard_map/all_gather | solution.py:123
  739.9 9.5 %convolution_convert_fusion = bf16[384,2048]{1,0:T(8,128)(2,1)} fusion(bf16[1024,2048]{1,0:T(8,128)(2,1)} %all-gather.23.cloned.1.call-done, f32[48,8,8,128]{3,2,1,0:T(8,128)S(1)} %bitcast.86, bf16[2048,1024]{1,0:T(8,128)(2,1)} %all-gather.21.cloned.1.call-done, f32[384,2048]{1,0:T(8,128)} %copy-done.3, f32[384]{0:T(512)S(1)} %add_rsqrt_fusion, ...), kind=kOutput, calls=%fused_computation.14 | convolution fusion | flops 3226730496 | bytes 14683136 | tf_op jit(solution)/shard_map/dot_general | solution.py:121
  749.4 69.5 %all-reduce.8.cloned.1.call-done = bf16[384,2048]{1,0:T(8,128)(2,1)} async-done(((bf16[384,2048]{1,0:T(8,128)(2,1)}), bf16[384,2048]{1,0:T(8,128)(2,1)}) %all-reduce.8.cloned.1.call-update) | async-done | bytes 1572880 | tf_op jit(solution)/shard_map/psum | solution.py:36
  (57 shorter events, 16.2 us)
Async XLA Ops:
  6.5 78.0 %copy-start = (bf16[384,256]{1,0:T(8,128)(2,1)S(1)}, bf16[384,256]{1,0:T(8,128)(2,1)}, u32[]{:S(2)}) copy-start(bf16[384,256]{1,0:T(8,128)(2,1)} %param.13) | copy-start | bytes 589828
  6.5 78.0 %all-gather.9.cloned.1.call-start = ((), (), s32[]{:S(2)}) async-start(), calls=%async_computation | async-start | bytes 3342336 | tf_op jit(solution)/shard_map/all_gather | solution.py:59
  8.3 149.3 %all-gather.11.cloned.1.call-start = ((), (), s32[]{:S(2)}) async-start(), calls=%async_computation.1 | async-start | bytes 3342336 | tf_op jit(solution)/shard_map/all_gather | solution.py:60
  9.1 213.1 %all-gather.13.cloned.1.call-start = ((), (), s32[]{:S(2)}) async-start(), calls=%async_computation.2 | async-start | bytes 1114112 | tf_op jit(solution)/shard_map/all_gather | solution.py:84
  9.8 284.6 %all-reduce.4.cloned.1.call-start = ((), (), s32[]{:S(2)}) async-start(), calls=%async_computation.3 | async-start | bytes 3145728 | tf_op jit(solution)/shard_map/psum | solution.py:36
  182.5 44.8 %copy-start.4 = (f32[31,256]{1,0:T(8,128)S(1)}, f32[31,256]{1,0:T(8,128)}, u32[]{:S(2)}) copy-start(f32[31,256]{1,0:T(8,128)} %param.19) | copy-start | bytes 95236
  182.6 111.8 %copy-start.1 = (bf16[384,2048]{1,0:T(8,128)(2,1)S(1)}, bf16[384,2048]{1,0:T(8,128)(2,1)}, u32[]{:S(2)}) copy-start(bf16[384,2048]{1,0:T(8,128)(2,1)} %param.12) | copy-start | bytes 4718596
  225.2 138.4 %all-gather.17.cloned.1.call-start = ((), (), s32[]{:S(2)}) async-start(), calls=%async_computation.5 | async-start | bytes 1114112 | tf_op jit(solution)/shard_map/all_gather | solution.py:94
  225.8 205.8 %all-gather.15.cloned.1.call-start = ((), (), s32[]{:S(2)}) async-start(), calls=%async_computation.4 | async-start | bytes 1114112 | tf_op jit(solution)/shard_map/all_gather | solution.py:93
  226.4 269.7 %all-gather.19.cloned.1.call-start = ((), (), s32[]{:S(2)}) async-start(), calls=%async_computation.6 | async-start | bytes 1114112 | tf_op jit(solution)/shard_map/all_gather | solution.py:109
  227.1 349.0 %all-reduce.6.cloned.1.call-start = ((), (), s32[]{:S(2)}) async-start(), calls=%async_computation.7 | async-start | bytes 3145728 | tf_op jit(solution)/shard_map/psum | solution.py:36
  294.4 2.0 copy-start.2
  434.0 8.0 copy-start.6
  434.0 62.1 %collective-permute-start = (bf16[15,256]{1,0:T(8,128)(2,1)S(1)}, bf16[15,256]{1,0:T(8,128)(2,1)S(1)}, u32[]{:S(2)}, u32[]{:S(2)}) collective-permute-start(bf16[15,256]{1,0:T(8,128)(2,1)S(1)} %get-tuple-element.7), channel_id=1, source_target_pairs={{0,16},{16,32},{32,48},{48,64},{64,80},{80,96},{96,112},{112,128},... | collective-permute-start | bytes 23048 | tf_op jit(solution)/shard_map/ppermute | solution.py:18
  436.5 59.6 %collective-permute-start.1 = (bf16[15,256]{1,0:T(8,128)(2,1)S(1)}, bf16[15,256]{1,0:T(8,128)(2,1)S(1)}, u32[]{:S(2)}, u32[]{:S(2)}) collective-permute-start(bf16[15,256]{1,0:T(8,128)(2,1)S(1)} %get-tuple-element.8), channel_id=1, source_target_pairs={{16,0},{32,16},{48,32},{64,48},{80,64},{96,80},{112,96},{128,112},... | collective-permute-start | bytes 23048 | tf_op jit(solution)/shard_map/ppermute | solution.py:19
  496.1 12.3 %copy-start.5 = (s32[3,8]{1,0:T(4,128)S(1)}, s32[3,8]{1,0:T(4,128)}, u32[]{:S(2)}) copy-start(s32[3,8]{1,0:T(4,128)} %param.23) | copy-start | bytes 292
  507.0 145.7 %all-gather.21.cloned.1.call-start = ((), (), s32[]{:S(2)}) async-start(), calls=%async_computation.8 | async-start | bytes 4456448 | tf_op jit(solution)/shard_map/all_gather | solution.py:114
  507.7 232.0 %all-gather.23.cloned.1.call-start = ((), (), s32[]{:S(2)}) async-start(), calls=%async_computation.9 | async-start | bytes 4456448 | tf_op jit(solution)/shard_map/all_gather | solution.py:123
  508.3 310.6 %all-reduce.8.cloned.1.call-start = ((), (), s32[]{:S(2)}) async-start(), calls=%async_computation.10 | async-start | bytes 3145728 | tf_op jit(solution)/shard_map/psum | solution.py:36
  578.3 1.7 copy-start.3
Sparse Core Ops, SparseCore 0:
  9.1 75.3 all-gather.8
  86.3 71.3 all-gather.10
  159.4 62.7 all-gather.12
  225.3 69.0 all-reduce.3
  296.0 67.5 all-gather.16
  365.3 66.3 all-gather.14
  433.3 62.6 all-gather.18
  507.1 69.0 all-reduce.5
  578.0 74.6 all-gather.20
  654.2 85.4 all-gather.22
  749.5 69.3 all-reduce.7
where the time goes:
time: 830 us
  waiting for transfers between devices  728 us (88%)
  matrix products  50.9 us (6%)
  other arithmetic  21 us (3%)
  between operations  13.4 us (2%)
  starting transfers between devices  8.53 us (1%)
  local copies, waits for them, and re-layouts  8.4 us (1%)
    psum x3, waiting for transfers between devices, add_branch(): lax.psum(branch_part.astype(jnp.bfloat16), 'mp').astype(jnp.float32)  204 us
    all_gather x1, waiting for transfers between devices, on_device(): lax.all_gather(ffn_down, 'seq', axis=1, tiled=True)  87.1 us
    all_gather x1, waiting for transfers between devices, on_device(): lax.all_gather(keys, 'seq', axis=0, tiled=True)  74.6 us
    all_gather x1, waiting for transfers between devices, on_device(): lax.all_gather(ffn_in, 'seq', axis=0, tiled=True)  72.2 us
    all_gather x1, waiting for transfers between devices, on_device(): lax.all_gather(conv_value, 'seq', axis=0, tiled=True)  65 us
    all_gather x1, waiting for transfers between devices, on_device(): lax.all_gather(conv_gate, 'seq', axis=0, tiled=True)  64.7 us
    all_gather x1, waiting for transfers between devices, on_device(): lax.all_gather(values, 'seq', axis=0, tiled=True)  61.8 us
    all_gather x1, waiting for transfers between devices, on_device(): lax.all_gather(conv_out, 'seq', axis=1, tiled=True)  54.1 us
  transfers between devices with their start and end apart: 13, of which 11 were waited for; matrix products, arithmetic and copies ran while one was open for 6% of the time, Pallas kernels for 0%

commit v1 on v0

--- a/solution.py
+++ b/solution.py
@@ -6,6 +6,13 @@
 
 HEAD_DIM = 128
 norm_epsilon = 1e-05
+
+
+def swapped_in(array, mesh_axis, along):
+    n_dev = lax.axis_size(mesh_axis)
+    pieces = jnp.stack([array for _ in range(n_dev)])
+    pieces = lax.all_to_all(pieces, mesh_axis, split_axis=0, concat_axis=0)
+    return jnp.concatenate(pieces, axis=along)
 
 
 def padded_2(value, sides, width):
@@ -105,9 +112,7 @@
         ].astype(jnp.float32)
     activated = jax.nn.silu(depth_out).astype(jnp.bfloat16)
     conv_part = jnp.dot(
-        activated,
-        lax.all_gather(conv_out, "seq", axis=1, tiled=True),
-        preferred_element_type=jnp.float32,
+        activated, swapped_in(conv_out, "seq", 1), preferred_element_type=jnp.float32
     )
     stream = add_branch(stream, conv_part, 1.0)
     norm_two = layer_norm(stream).astype(jnp.bfloat16)

time: 830 us -> 779 us (0.939)
  waiting for transfers between devices: 728 us -> 671 us
    all_gather x1 -> x0, waiting for transfers between devices: 54.1 us -> none  [on_device(): lax.all_gather(conv_out, 'seq', axis=1, tiled=True)]
where the time goes in v1:
time: 779 us; the launch traced here: 778 us
  waiting for transfers between devices  671 us (86%)
  matrix products  49.8 us (6%)
  other arithmetic  21 us (3%)
  starting transfers between devices  14.9 us (2%)
  between operations  13.7 us (2%)
  local copies, waits for them, and re-layouts  8.09 us (1%)
    psum x3, waiting for transfers between devices, add_branch(): lax.psum(branch_part.astype(jnp.bfloat16), 'mp').astype(jnp.float32)  198 us
    all_gather x1, waiting for transfers between devices, on_device(): lax.all_gather(ffn_down, 'seq', axis=1, tiled=True)  87.2 us
    all_gather x1, waiting for transfers between devices, on_device(): lax.all_gather(keys, 'seq', axis=0, tiled=True)  74.6 us
    all_gather x1, waiting for transfers between devices, on_device(): lax.all_gather(ffn_in, 'seq', axis=0, tiled=True)  72.2 us
    all_gather x1, waiting for transfers between devices, on_device(): lax.all_gather(conv_value, 'seq', axis=0, tiled=True)  65 us
    all_gather x1, waiting for transfers between devices, on_device(): lax.all_gather(conv_gate, 'seq', axis=0, tiled=True)  64.7 us
    all_gather x1, waiting for transfers between devices, on_device(): lax.all_gather(values, 'seq', axis=0, tiled=True)  61.8 us
    all_gather x1, waiting for transfers between devices, on_device(): lax.all_gather(w_out, 'seq', axis=1, tiled=True)  42.1 us
  transfers between devices with their start and end apart: 13, of which 11 were waited for; matrix products, arithmetic and copies ran while one was open for 6% of the time, Pallas kernels for 0%

profile of v1, /device:TPU:2, one launch (start us, length us, event | category | flops | bytes accessed | tf_op | source)
XLA Modules:
  0.0 778.3 jit_solution(5712600199504699896)
XLA Ops:
  9.9 74.6 %all-gather.8.cloned.1.call-done = bf16[6144,256]{0,1:T(8,128)(2,1)} async-done(((bf16[384,256]{0,1:T(8,128)(2,1)}), bf16[6144,256]{0,1:T(8,128)(2,1)}) %all-gather.8.cloned.1.call-update) | async-done | bytes 3145744 | tf_op jit(solution)/shard_map/all_gather | solution.py:66
  84.5 11.3 %bitcast_reduce_fusion = (f32[384,2]{0,1:T(2,128)S(1)}, f32[2,6144,384]{2,1,0:T(8,128)}) fusion(bf16[6144,2,128]{0,2,1:T(8,128)(2,1)} %bitcast.88, bf16[384,256]{1,0:T(8,128)(2,1)S(1)} %copy-done), kind=kOutput, calls=%fused_computation.1 | convolution fusion | flops 1217395968 | bytes 22219776 | tf_op jit(solution)/shard_map/qhd,khd->qhk/dot_general | solution.py:73
  95.8 61.8 %all-gather.10.cloned.1.call-done = bf16[6144,256]{1,0:T(8,128)(2,1)} async-done(((bf16[384,256]{1,0:T(8,128)(2,1)}), bf16[6144,256]{1,0:T(8,128)(2,1)}) %all-gather.10.cloned.1.call-update) | async-done | bytes 3145744 | tf_op jit(solution)/shard_map/all_gather | solution.py:67
  157.6 3.2 copy.19
  160.8 9.4 %fusion.1 = f32[384,2]{0,1:T(2,128)S(1)} fusion(f32[2,6144,384]{2,1,0:T(8,128)} %get-tuple-element.41, f32[384,2]{0,1:T(2,128)S(1)} %broadcast_maximum_fusion), kind=kLoop, calls=%fused_computation.3 | loop fusion | flops 14155008 | bytes 18880512 | tf_op jit(solution)/shard_map/reduce_sum | solution.py:78
  170.3 9.8 %fusion.22 = bf16[384,2,128]{0,2,1:T(8,128)(2,1)S(1)} fusion(bf16[6144,2,128]{0,2,1:T(8,128)(2,1)S(1)} %bitcast.87, f32[2,6144,384]{2,1,0:T(8,128)} %get-tuple-element.41, f32[384,2]{0,1:T(2,128)S(1)} %broadcast_maximum_fusion, f32[384,2]{0,1:T(2,128)S(1)} %fusion.1), kind=kOutput, calls=%fused_computation.59 | convolution fusion | flops 1222311936 | bytes 22222848 | tf_op jit(solution)/shard_map/qhk,khd->qhd/dot_general | solution.py:79
  180.1 42.1 %all-gather.12.cloned.1.call-done = bf16[256,2048]{1,0:T(8,128)(2,1)} async-done(((bf16[256,128]{1,0:T(8,128)(2,1)}), bf16[256,2048]{1,0:T(8,128)(2,1)}) %all-gather.12.cloned.1.call-update) | async-done | bytes 1048592 | tf_op jit(solution)/shard_map/all_gather | solution.py:91
  222.2 3.0 convolution_convert_fusion.2
  227.0 6.4 all-to-all-start
  234.2 60.6 %all-reduce.4.cloned.1.call-done = bf16[384,2048]{1,0:T(8,128)(2,1)} async-done(((bf16[384,2048]{1,0:T(8,128)(2,1)}), bf16[384,2048]{1,0:T(8,128)(2,1)}) %all-reduce.4.cloned.1.call-update) | async-done | bytes 1572880 | tf_op jit(solution)/shard_map/psum | solution.py:43
  294.9 2.0 fusion.7
  299.4 64.7 %all-gather.16.cloned.1.call-done = bf16[2048,256]{1,0:T(8,128)(2,1)} async-done(((bf16[128,256]{1,0:T(8,128)(2,1)}), bf16[2048,256]{1,0:T(8,128)(2,1)}) %all-gather.16.cloned.1.call-update) | async-done | bytes 1048592 | tf_op jit(solution)/shard_map/all_gather | solution.py:101
  364.1 3.0 fusion.14
  367.1 65.0 %all-gather.14.cloned.1.call-done = bf16[2048,256]{1,0:T(8,128)(2,1)} async-done(((bf16[128,256]{1,0:T(8,128)(2,1)}), bf16[2048,256]{1,0:T(8,128)(2,1)}) %all-gather.14.cloned.1.call-update) | async-done | bytes 1048592 | tf_op jit(solution)/shard_map/all_gather | solution.py:100
  432.1 2.4 fusion.18
  434.5 2.5 collective-permute-start
  436.9 5.5 collective-permute-start.1
  443.8 10.8 %convolution_convert_fusion.1 = bf16[384,2048]{1,0:T(8,128)(2,1)} fusion(bf16[256,2048]{0,1:T(8,128)(2,1)} %bitcast.37, bf16[384,256]{1,0:T(8,128)(2,1)} %copy-done.7, bf16[15,256]{1,0:T(8,128)(2,1)S(1)} %collective-permute-done.1, bf16[15,256]{1,0:T(8,128)(2,1)S(1)} %collective-permute-done, f32[256]{0:T(256)S(1)} %bitcast.120, f32[256]{0:T(256)S(1)} %bitcast.121, ...), kind=kOutput, calls=%fused_computation.15 | convolution fusion | flops 421822464 | bytes 2865152 | tf_op jit(solution)/shard_map/dot_general | solution.py:114
  456.2 67.8 %all-reduce.6.cloned.1.call-done = bf16[384,2048]{1,0:T(8,128)(2,1)} async-done(((bf16[384,2048]{1,0:T(8,128)(2,1)}), bf16[384,2048]{1,0:T(8,128)(2,1)}) %all-reduce.6.cloned.1.call-update) | async-done | bytes 1572880 | tf_op jit(solution)/shard_map/psum | solution.py:43
  524.0 2.1 fusion.61
  528.3 72.2 %all-gather.18.cloned.1.call-done = bf16[2048,1024]{1,0:T(8,128)(2,1)} async-done(((bf16[128,1024]{1,0:T(8,128)(2,1)}), bf16[2048,1024]{1,0:T(8,128)(2,1)}) %all-gather.18.cloned.1.call-update) | async-done | bytes 4194320 | tf_op jit(solution)/shard_map/all_gather | solution.py:119
  600.5 87.2 %all-gather.20.cloned.1.call-done = bf16[1024,2048]{1,0:T(8,128)(2,1)} async-done(((bf16[1024,128]{1,0:T(8,128)(2,1)}), bf16[1024,2048]{1,0:T(8,128)(2,1)}) %all-gather.20.cloned.1.call-update) | async-done | bytes 4194320 | tf_op jit(solution)/shard_map/all_gather | solution.py:128
  687.9 9.4 %convolution_convert_fusion = bf16[384,2048]{1,0:T(8,128)(2,1)} fusion(bf16[1024,2048]{1,0:T(8,128)(2,1)} %all-gather.20.cloned.1.call-done, f32[48,8,8,128]{3,2,1,0:T(8,128)S(1)} %bitcast.89, bf16[2048,1024]{1,0:T(8,128)(2,1)} %all-gather.18.cloned.1.call-done, f32[384,2048]{1,0:T(8,128)} %copy-done.3, f32[384]{0:T(512)S(1)} %add_rsqrt_fusion, ...), kind=kOutput, calls=%fused_computation.14 | convolution fusion | flops 3226730496 | bytes 14683136 | tf_op jit(solution)/shard_map/dot_general | solution.py:126
  697.4 69.5 %all-reduce.8.cloned.1.call-done = bf16[384,2048]{1,0:T(8,128)(2,1)} async-done(((bf16[384,2048]{1,0:T(8,128)(2,1)}), bf16[384,2048]{1,0:T(8,128)(2,1)}) %all-reduce.8.cloned.1.call-update) | async-done | bytes 1572880 | tf_op jit(solution)/shard_map/psum | solution.py:43
  (60 shorter events, 18.1 us)
Async XLA Ops:
  6.5 78.0 %copy-start = (bf16[384,256]{1,0:T(8,128)(2,1)S(1)}, bf16[384,256]{1,0:T(8,128)(2,1)}, u32[]{:S(2)}) copy-start(bf16[384,256]{1,0:T(8,128)(2,1)} %param.13) | copy-start | bytes 589828
  6.5 78.0 %all-gather.8.cloned.1.call-start = ((), (), s32[]{:S(2)}) async-start(), calls=%async_computation.1 | async-start | bytes 3342336 | tf_op jit(solution)/shard_map/all_gather | solution.py:66
  8.3 149.3 %all-gather.10.cloned.1.call-start = ((), (), s32[]{:S(2)}) async-start(), calls=%async_computation.2 | async-start | bytes 3342336 | tf_op jit(solution)/shard_map/all_gather | solution.py:67
  9.1 213.1 %all-gather.12.cloned.1.call-start = ((), (), s32[]{:S(2)}) async-start(), calls=%async_computation.3 | async-start | bytes 1114112 | tf_op jit(solution)/shard_map/all_gather | solution.py:91
  9.8 285.0 %all-reduce.4.cloned.1.call-start = ((), (), s32[]{:S(2)}) async-start(), calls=%async_computation.4 | async-start | bytes 3145728 | tf_op jit(solution)/shard_map/psum | solution.py:43
  180.1 45.7 %copy-start.4 = (bf16[256,128]{1,0:T(8,128)(2,1)S(1)}, bf16[256,128]{1,0:T(8,128)(2,1)}, u32[]{:S(2)}) copy-start(bf16[256,128]{1,0:T(8,128)(2,1)} %param.20) | copy-start | bytes 196612
  225.2 9.0 %copy-start.5 = (f32[31,256]{1,0:T(8,128)S(1)}, f32[31,256]{1,0:T(8,128)}, u32[]{:S(2)}) copy-start(f32[31,256]{1,0:T(8,128)} %param.19) | copy-start | bytes 95236
  225.2 69.7 %copy-start.1 = (bf16[384,2048]{1,0:T(8,128)(2,1)S(1)}, bf16[384,2048]{1,0:T(8,128)(2,1)}, u32[]{:S(2)}) copy-start(bf16[384,2048]{1,0:T(8,128)(2,1)} %param.12) | copy-start | bytes 4718596
  225.2 138.9 %all-gather.16.cloned.1.call-start = ((), (), s32[]{:S(2)}) async-start(), calls=%async_computation.6 | async-start | bytes 1114112 | tf_op jit(solution)/shard_map/all_gather | solution.py:101
  227.0 215.5 %all-to-all-start = ((bf16[16,256,128]{1,2,0:T(8,128)(2,1)}), bf16[16,256,128]{1,2,0:T(8,128)(2,1)}, u32[]{:S(2)}, u32[]{:S(2)}) async-start(bf16[16,256,128]{1,2,0:T(8,128)(2,1)} %stack.2), calls=%async_computation | async-start | bytes 2097152 | tf_op jit(solution)/shard_map/all_to_all | solution.py:14
  233.4 198.7 %all-gather.14.cloned.1.call-start = ((), (), s32[]{:S(2)}) async-start(), calls=%async_computation.5 | async-start | bytes 1114112 | tf_op jit(solution)/shard_map/all_gather | solution.py:100
  233.9 290.0 %all-reduce.6.cloned.1.call-start = ((), (), s32[]{:S(2)}) async-start(), calls=%async_computation.7 | async-start | bytes 3145728 | tf_op jit(solution)/shard_map/psum | solution.py:43
  294.9 2.0 copy-start.2
  434.4 8.0 %copy-start.7 = (bf16[384,256]{1,0:T(8,128)(2,1)}, bf16[384,256]{1,0:T(8,128)(2,1)S(1)}, u32[]{:S(2)}) copy-start(bf16[384,256]{1,0:T(8,128)(2,1)S(1)} %fusion.18) | copy-start | bytes 589828
  434.5 8.0 %collective-permute-start = (bf16[15,256]{1,0:T(8,128)(2,1)S(1)}, bf16[15,256]{1,0:T(8,128)(2,1)S(1)}, u32[]{:S(2)}, u32[]{:S(2)}) collective-permute-start(bf16[15,256]{1,0:T(8,128)(2,1)S(1)} %get-tuple-element.7), channel_id=1, source_target_pairs={{0,16},{16,32},{32,48},{48,64},{64,80},{80,96},{96,112},{112,128},... | collective-permute-start | bytes 23048 | tf_op jit(solution)/shard_map/ppermute | solution.py:25
  436.9 6.8 collective-permute-start.1
  443.8 12.4 %copy-start.6 = (s32[3,8]{1,0:T(4,128)S(1)}, s32[3,8]{1,0:T(4,128)}, u32[]{:S(2)}) copy-start(s32[3,8]{1,0:T(4,128)} %param.23) | copy-start | bytes 292
  454.6 145.8 %all-gather.18.cloned.1.call-start = ((), (), s32[]{:S(2)}) async-start(), calls=%async_computation.8 | async-start | bytes 4456448 | tf_op jit(solution)/shard_map/all_gather | solution.py:119
  455.4 232.3 %all-gather.20.cloned.1.call-start = ((), (), s32[]{:S(2)}) async-start(), calls=%async_computation.9 | async-start | bytes 4456448 | tf_op jit(solution)/shard_map/all_gather | solution.py:128
  456.1 310.7 %all-reduce.8.cloned.1.call-start = ((), (), s32[]{:S(2)}) async-start(), calls=%async_computation.10 | async-start | bytes 3145728 | tf_op jit(solution)/shard_map/psum | solution.py:43
  526.1 1.7 copy-start.3
Sparse Core Ops, SparseCore 0:
  9.1 75.3 all-gather.7
  86.3 71.3 all-gather.9
  159.4 62.7 all-gather.11
  225.3 69.4 all-reduce.3
  296.5 67.5 all-gather.15
  365.7 66.3 all-gather.13
  454.8 69.1 all-reduce.5
  525.8 74.6 all-gather.17
  602.2 85.4 all-gather.19
  697.5 69.3 all-reduce.7
